TPU v7x, 32 devices: a whole 2x2x4 slice. The times are simulated.
32 devices in a mesh: dp: 8 (over z, y), mp: 4 (over x, core).
Axes of the slice: x: 2, y: 2, z: 4, core: 2. Of those that a mesh axis runs over, the one named last changes fastest.
Arguments:
- tokens: bfloat16 [8192, 2048], P('dp'), may hold values from -6 to 6
- documents: int32 [8, 1024], P('dp'), may hold values from 0 to 3, never falling along the last dimension, each value on 1 to 512 neighbouring positions
- cotangent: bfloat16 [8192, 2048], P('dp'), may hold values from -6 to 6
- attn_gain: float32 [2048], P('dp'), may hold values from 0.5 to 1.5
- query_gain: float32 [128], P('dp'), may hold values from 1 to 2
- key_norm_scale: float32 [128], P('dp'), may hold values from 0.25 to 1.75
- query_weight: float32 [2048, 2048], P('dp', 'mp'), may hold values from -0.125 to 0.125
- key_projection: float32 [2048, 1024], P('dp', 'mp'), may hold values from -0.125 to 0.125
- value_projection: float32 [2048, 1024], P('dp', 'mp'), may hold values from -0.125 to 0.125
- output_weight: float32 [2048, 2048], P('mp', 'dp'), may hold values from -1 to 1
- mlp_gain: float32 [2048], P('dp'), may hold values from 0.5 to 1.5
- gate_weight: float32 [2048, 6144], P('dp', 'mp'), may hold values from -0.125 to 0.125
- up_weight: float32 [2048, 6144], P('dp', 'mp'), may hold values from -0.125 to 0.125
- down_weight: float32 [6144, 2048], P('mp', 'dp'), may hold values from -0.078125 to 0.078125
Outputs:
- layer_output: bfloat16 [8192, 2048], P(('dp', 'mp'))
- input_grad: float32 [8192, 2048], P(('dp', 'mp'))
- attn_gain_grad: float32 [2048], P('dp')
- query_gain_grad: float32 [128], P('dp')
- key_gain_grad: float32 [128], P('dp')
- query_weight_grad: float32 [2048, 2048], P('dp', 'mp')
- key_weight_grad: float32 [2048, 1024], P('dp', 'mp')
- value_weight_grad: float32 [2048, 1024], P('dp', 'mp')
- output_weight_grad: float32 [2048, 2048], P('mp', 'dp')
- mlp_gain_grad: float32 [2048], P('dp')
- gate_weight_grad: float32 [2048, 6144], P('dp', 'mp')
- up_weight_grad: float32 [2048, 6144], P('dp', 'mp')
- down_weight_grad: float32 [6144, 2048], P('mp', 'dp')
Inputs may be any that keep to these rules, and one draw needn't show every extreme that they name: `documents`: document numbers never fall along a sequence; each document holds 1 to 512 positions, and some document holds exactly 512.
All inputs are finite; a program needn't handle non-finite values.
Results may differ from a plain program's by a relative error of at most 0.023.
Values may be sent and summed in bfloat16 or wider, within the bound.
A program may use at most 256 MiB of HBM per device.

v0:
```python
import jax
import jax.numpy as jnp
from jax import lax
from jax.sharding import PartitionSpec as P

QUERY_HEADS = 16
KEY_VALUE_HEADS = 8
HEAD_WIDTH = 128
EPSILON = 1e-06
MASKED = -1e30


def doc_positions(documents):
    indices = jnp.arange(documents.shape[-1], dtype=jnp.int32)
    boundary = jnp.concatenate(
        [
            jnp.ones(documents.shape[:-1] + (1,), dtype=jnp.bool_),
            documents[:, 1:] != documents[:, :-1],
        ],
        -1,
    )
    starts = lax.cummax(jnp.where(boundary, indices[None, :], 0), axis=1)
    return indices[None, :] - starts


def rope_tables(positions, head_size):
    middle = head_size // 2
    frequency = jnp.power(1000000.0, -2.0 * jnp.arange(middle, dtype=jnp.float32) / head_size)
    angles = positions.astype(jnp.float32)[:, None] * frequency[None, :]
    cosine_table = jnp.cos(angles)
    sine_table = jnp.sin(angles)
    return (
        jnp.concatenate([cosine_table, cosine_table], -1),
        jnp.concatenate([sine_table, sine_table], -1),
    )


def rotate(values):
    middle = values.shape[-1] // 2
    return jnp.concatenate([-values[..., middle:], values[..., :middle]], -1)


def rotate_back(values):
    middle = values.shape[-1] // 2
    return jnp.concatenate([values[..., middle:], -values[..., :middle]], -1)


def norm_parts(values):
    scaling = lax.rsqrt(jnp.mean(values * values, -1, keepdims=True) + EPSILON)
    return (values * scaling, scaling)


def norm_back(grad_normed, normed_hat, scaling, gains):
    scaled = grad_normed * gains
    return scaling * (scaled - normed_hat * jnp.mean(scaled * normed_hat, -1, keepdims=True))


def contract_rows(left, right):
    return lax.dot_general(
        left, right, (((0,), (0,)), ((), ())), preferred_element_type=jnp.float32
    )


def contract_cols(left, right):
    return lax.dot_general(
        left, right, (((1,), (1,)), ((), ())), preferred_element_type=jnp.float32
    )


def block_scores(query_rows, key_token_rows, doc_row, start, width, factor):
    scores = (
        jnp.einsum("qgrd,kgd->grqk", query_rows, key_token_rows, preferred_element_type=jnp.float32)
        * factor
    )
    query_index = start + jnp.arange(width)
    key_index = jnp.arange(key_token_rows.shape[0])
    allowed = (doc_row[start : start + width, None] == doc_row[None, :]) & (
        key_index[None, :] <= query_index[:, None]
    )
    return jnp.where(allowed, scores, MASKED)


def on_device(
    tokens,
    documents,
    cotangent,
    attn_gain,
    query_gain,
    key_norm_scale,
    query_weight,
    key_projection,
    value_projection,
    output_weight,
    mlp_gain,
    gate_weight,
    up_weight,
    down_weight,
):
    rows = tokens.shape[0]
    seqs, seq_length = documents.shape
    head_size = HEAD_WIDTH
    local_heads = QUERY_HEADS // lax.axis_size("mp")
    device_groups = KEY_VALUE_HEADS // lax.axis_size("mp")
    query_group = QUERY_HEADS // KEY_VALUE_HEADS
    block = min(512, seq_length)
    factor = head_size ** (-0.5)
    share = rows // lax.axis_size("mp")
    offset = lax.axis_index("mp") * share

    def take(values):
        return lax.dynamic_slice_in_dim(values, offset, share, 0)

    attn_parts = (
        lax.all_gather(attn_gain.astype(jnp.bfloat16), "dp", axis=0, tiled=True),
        lax.all_gather(query_gain.astype(jnp.bfloat16), "dp", axis=0, tiled=True),
        lax.all_gather(key_norm_scale.astype(jnp.bfloat16), "dp", axis=0, tiled=True),
        lax.all_gather(query_weight.astype(jnp.bfloat16), "dp", axis=0, tiled=True),
        lax.all_gather(key_projection.astype(jnp.bfloat16), "dp", axis=0, tiled=True),
        lax.all_gather(value_projection.astype(jnp.bfloat16), "dp", axis=0, tiled=True),
        lax.all_gather(output_weight.astype(jnp.bfloat16), "dp", axis=1, tiled=True),
    )
    gain_one = attn_parts[0].astype(jnp.float32)
    gain_query = attn_parts[1].astype(jnp.float32)
    gain_key = attn_parts[2].astype(jnp.float32)
    query_mat, key_mat, value_mat, output_mat = (
        attn_parts[3],
        attn_parts[4],
        attn_parts[5],
        attn_parts[6],
    )
    mlp_parts = (
        lax.all_gather(mlp_gain.astype(jnp.bfloat16), "dp", axis=0, tiled=True),
        lax.all_gather(gate_weight.astype(jnp.bfloat16), "dp", axis=0, tiled=True),
        lax.all_gather(up_weight.astype(jnp.bfloat16), "dp", axis=0, tiled=True),
        lax.all_gather(down_weight.astype(jnp.bfloat16), "dp", axis=1, tiled=True),
    )
    gain_two = mlp_parts[0].astype(jnp.float32)
    gate_mat, up_mat, down_mat = (mlp_parts[1], mlp_parts[2], mlp_parts[3])
    inputs = tokens.astype(jnp.float32)
    hat_one, inv_one = norm_parts(inputs)
    normed_one = (hat_one * gain_one).astype(jnp.bfloat16)
    query_raw = jnp.dot(normed_one, query_mat, preferred_element_type=jnp.float32)
    key_unnormed = jnp.dot(normed_one, key_mat, preferred_element_type=jnp.float32)
    value_token_rows = jnp.dot(normed_one, value_mat, preferred_element_type=jnp.float32).astype(
        jnp.bfloat16
    )
    positions = doc_positions(documents).reshape(rows)
    cosine_table, sine_table = rope_tables(positions, head_size)
    cosine_table = cosine_table[:, None, :]
    sine_table = sine_table[:, None, :]
    query_hat, query_inv = norm_parts(query_raw.reshape(rows, local_heads, head_size))
    key_hat, key_inv = norm_parts(key_unnormed.reshape(rows, device_groups, head_size))
    query_normed = query_hat * gain_query
    key_normed = key_hat * gain_key
    query_rows = (query_normed * cosine_table + rotate(query_normed) * sine_table).astype(
        jnp.bfloat16
    )
    key_token_rows = (key_normed * cosine_table + rotate(key_normed) * sine_table).astype(
        jnp.bfloat16
    )
    query_seq = query_rows.reshape(seqs, seq_length, device_groups, query_group, head_size)
    key_seq = key_token_rows.reshape(seqs, seq_length, device_groups, head_size)
    value_seq = value_token_rows.reshape(seqs, seq_length, device_groups, head_size)

    def attend_forward(items):
        seq_queries, seq_keys, seq_values, doc_row = items
        outputs = []
        log_totals = []
        for start in range(0, seq_length, block):
            scores = block_scores(
                seq_queries[start : start + block], seq_keys, doc_row, start, block, factor
            )
            highest = jnp.max(scores, -1, keepdims=True)
            exponent = jnp.exp(scores - highest)
            totals = jnp.sum(exponent, -1, keepdims=True)
            weights_block = (exponent / totals).astype(jnp.bfloat16)
            outputs.append(
                jnp.einsum(
                    "grqk,kgd->qgrd", weights_block, seq_values, preferred_element_type=jnp.float32
                )
            )
            log_totals.append(highest + jnp.log(totals))
        return (jnp.concatenate(outputs, 0), jnp.concatenate(log_totals, 2))

    attention_output, log_total = lax.map(
        attend_forward, (query_seq, key_seq, value_seq, documents)
    )
    attended_flat = attention_output.reshape(rows, local_heads * head_size).astype(jnp.bfloat16)
    attn_part = jnp.dot(attended_flat, output_mat, preferred_element_type=jnp.float32)
    hidden = inputs + lax.psum(attn_part, "mp")
    hat_two, inv_two = norm_parts(hidden)
    normed_two = (hat_two * gain_two).astype(jnp.bfloat16)
    hidden_share = take(hidden)
    gate_pre = jnp.dot(normed_two, gate_mat, preferred_element_type=jnp.float32)
    up_pre = jnp.dot(normed_two, up_mat, preferred_element_type=jnp.float32)
    sigmoid = jax.nn.sigmoid(gate_pre)
    swish = gate_pre * sigmoid
    active = (swish * up_pre).astype(jnp.bfloat16)
    mlp_part = jnp.dot(active, down_mat, preferred_element_type=jnp.float32)
    layer_output = (
        hidden_share + take(lax.psum(mlp_part.astype(jnp.bfloat16), "mp").astype(jnp.float32))
    ).astype(jnp.bfloat16)
    back_gain_one, back_gain_query, back_gain_key = (gain_one, gain_query, gain_key)
    back_query, back_key, back_value, back_output = (query_mat, key_mat, value_mat, output_mat)
    back_gate, back_up, back_down = (gate_mat, up_mat, down_mat)
    grad_out = cotangent.astype(jnp.float32)
    grad_active = contract_cols(cotangent, back_down)
    down_grad = contract_rows(active, cotangent)
    grad_gate = (grad_active * up_pre * sigmoid * (1.0 + gate_pre * (1.0 - sigmoid))).astype(
        jnp.bfloat16
    )
    grad_up = (grad_active * swish).astype(jnp.bfloat16)
    gate_grad = contract_rows(normed_two, grad_gate)
    up_grad = contract_rows(normed_two, grad_up)
    normed_two_part = contract_cols(grad_gate, back_gate) + contract_cols(grad_up, back_up)
    normed_two_grad = lax.psum(normed_two_part.astype(jnp.bfloat16), "mp").astype(jnp.float32)
    mlp_gain_part = jnp.sum(normed_two_grad * hat_two, 0)
    grad_hidden = grad_out + norm_back(normed_two_grad, hat_two, inv_two, gain_two)
    grad_hidden_low = grad_hidden.astype(jnp.bfloat16)
    grad_hidden_share = take(grad_hidden)
    output_grad = contract_rows(attended_flat, grad_hidden_low)
    grad_attended = contract_cols(grad_hidden_low, back_output).astype(jnp.bfloat16)
    grad_attended_seq = grad_attended.reshape(
        seqs, seq_length, device_groups, query_group, head_size
    )

    def attend_backward(items):
        seq_queries, seq_keys, seq_values, doc_row, seq_log_total, seq_grad = items
        query_grads = []
        key_grad = jnp.zeros((seq_length, device_groups, head_size), jnp.float32)
        value_grad = jnp.zeros((seq_length, device_groups, head_size), jnp.float32)
        for start in range(0, seq_length, block):
            block_queries = seq_queries[start : start + block]
            block_grad = seq_grad[start : start + block]
            scores = block_scores(block_queries, seq_keys, doc_row, start, block, factor)
            weights_block = jnp.exp(scores - seq_log_total[:, :, start : start + block])
            grad_weights = jnp.einsum(
                "qgrd,kgd->grqk", block_grad, seq_values, preferred_element_type=jnp.float32
            )
            inner = jnp.sum(weights_block * grad_weights, -1, keepdims=True)
            grad_scores = (weights_block * (grad_weights - inner)).astype(jnp.bfloat16)
            query_grads.append(
                jnp.einsum(
                    "grqk,kgd->qgrd", grad_scores, seq_keys, preferred_element_type=jnp.float32
                )
                * factor
            )
            key_grad = (
                key_grad
                + jnp.einsum(
                    "grqk,qgrd->kgd", grad_scores, block_queries, preferred_element_type=jnp.float32
                )
                * factor
            )
            value_grad = value_grad + jnp.einsum(
                "grqk,qgrd->kgd",
                weights_block.astype(jnp.bfloat16),
                block_grad,
                preferred_element_type=jnp.float32,
            )
        return (jnp.concatenate(query_grads, 0), key_grad, value_grad)

    query_rot_grad, key_rot_grad, value_seq_grad = lax.map(
        attend_backward, (query_seq, key_seq, value_seq, documents, log_total, grad_attended_seq)
    )
    query_rot_grad = query_rot_grad.reshape(rows, local_heads, head_size)
    key_rot_grad = key_rot_grad.reshape(rows, device_groups, head_size)
    query_norm_grad = query_rot_grad * cosine_table + rotate_back(query_rot_grad * sine_table)
    key_norm_grad = key_rot_grad * cosine_table + rotate_back(key_rot_grad * sine_table)
    query_gain_part = jnp.sum(query_norm_grad * query_hat, (0, 1))
    key_gain_part = jnp.sum(key_norm_grad * key_hat, (0, 1))
    query_raw_grad = (
        norm_back(query_norm_grad, query_hat, query_inv, back_gain_query)
        .reshape(rows, local_heads * head_size)
        .astype(jnp.bfloat16)
    )
    key_raw_grad = (
        norm_back(key_norm_grad, key_hat, key_inv, back_gain_key)
        .reshape(rows, device_groups * head_size)
        .astype(jnp.bfloat16)
    )
    value_raw_grad = value_seq_grad.reshape(rows, device_groups * head_size).astype(jnp.bfloat16)
    query_grad = contract_rows(normed_one, query_raw_grad)
    key_grad = contract_rows(normed_one, key_raw_grad)
    value_grad = contract_rows(normed_one, value_raw_grad)
    normed_one_part = (
        contract_cols(query_raw_grad, back_query)
        + contract_cols(key_raw_grad, back_key)
        + contract_cols(value_raw_grad, back_value)
    )
    hat_one_share = take(hat_one)
    inv_one_share = take(inv_one)
    normed_one_grad, query_gain_sum, key_gain_sum = (
        lax.psum(normed_one_part.astype(jnp.bfloat16), "mp").astype(jnp.float32),
        lax.psum(query_gain_part.astype(jnp.bfloat16), "mp").astype(jnp.float32),
        lax.psum(key_gain_part.astype(jnp.bfloat16), "mp").astype(jnp.float32),
    )
    attn_gain_total = jnp.sum(normed_one_grad * hat_one, 0)
    input_grad = grad_hidden_share + norm_back(
        take(normed_one_grad), hat_one_share, inv_one_share, back_gain_one
    )
    attn_grads = (
        lax.psum_scatter(
            attn_gain_total.astype(jnp.bfloat16), "dp", scatter_dimension=0, tiled=True
        ).astype(jnp.float32),
        lax.psum_scatter(
            query_gain_sum.astype(jnp.bfloat16), "dp", scatter_dimension=0, tiled=True
        ).astype(jnp.float32),
        lax.psum_scatter(
            key_gain_sum.astype(jnp.bfloat16), "dp", scatter_dimension=0, tiled=True
        ).astype(jnp.float32),
        lax.psum_scatter(
            query_grad.astype(jnp.bfloat16), "dp", scatter_dimension=0, tiled=True
        ).astype(jnp.float32),
        lax.psum_scatter(
            key_grad.astype(jnp.bfloat16), "dp", scatter_dimension=0, tiled=True
        ).astype(jnp.float32),
        lax.psum_scatter(
            value_grad.astype(jnp.bfloat16), "dp", scatter_dimension=0, tiled=True
        ).astype(jnp.float32),
        lax.psum_scatter(
            output_grad.astype(jnp.bfloat16), "dp", scatter_dimension=1, tiled=True
        ).astype(jnp.float32),
    )
    mlp_grads = (
        lax.psum_scatter(
            mlp_gain_part.astype(jnp.bfloat16), "dp", scatter_dimension=0, tiled=True
        ).astype(jnp.float32),
        lax.psum_scatter(
            gate_grad.astype(jnp.bfloat16), "dp", scatter_dimension=0, tiled=True
        ).astype(jnp.float32),
        lax.psum_scatter(
            up_grad.astype(jnp.bfloat16), "dp", scatter_dimension=0, tiled=True
        ).astype(jnp.float32),
        lax.psum_scatter(
            down_grad.astype(jnp.bfloat16), "dp", scatter_dimension=1, tiled=True
        ).astype(jnp.float32),
    )
    return (
        layer_output,
        input_grad,
        attn_grads[0],
        attn_grads[1],
        attn_grads[2],
        attn_grads[3],
        attn_grads[4],
        attn_grads[5],
        attn_grads[6],
        mlp_grads[0],
        mlp_grads[1],
        mlp_grads[2],
        mlp_grads[3],
    )


def solution(mesh):
    in_specs = (
        P("dp", None),
        P("dp", None),
        P("dp", None),
        P("dp"),
        P("dp"),
        P("dp"),
        P("dp", "mp"),
        P("dp", "mp"),
        P("dp", "mp"),
        P("mp", "dp"),
        P("dp"),
        P("dp", "mp"),
        P("dp", "mp"),
        P("mp", "dp"),
    )
    out_specs = (
        P(("dp", "mp"), None),
        P(("dp", "mp"), None),
        P("dp"),
        P("dp"),
        P("dp"),
        P("dp", "mp"),
        P("dp", "mp"),
        P("dp", "mp"),
        P("mp", "dp"),
        P("dp"),
        P("dp", "mp"),
        P("dp", "mp"),
        P("mp", "dp"),
    )
    return jax.shard_map(
        on_device, mesh=mesh, in_specs=in_specs, out_specs=out_specs, check_vma=False
    )
```

profile of v0, /device:TPU:0, one launch (start us, length us, event | category | flops | bytes accessed | tf_op | source)
XLA Modules:
  0.0 1635.1 jit_solution(17745862805396485269)
XLA Ops:
  16.6 22.3 %all-gather = bf16[8,1,256]{2,1,0:T(2,128)(2,1)S(1)} all-gather(bf16[1,1,256]{2,1,0:T(2,128)(2,1)S(1)} %reshape.304), channel_id=1, replica_groups=mesh['dp'=8,'mp'=4] {'dp'}, dimensions={0}, use_global_device_ids=true | all-gather | bytes 4608 | tf_op jit(solution)/shard_map/all_gather | solution.py:114
  43.8 17.2 %all-reduce.7 = (bf16[128]{0:T(256)(128)(2,1)S(1)}, bf16[128]{0:T(256)(128)(2,1)S(1)}) all-reduce(bf16[128]{0:T(256)(128)(2,1)S(1)} %dynamic-update-slice, bf16[128]{0:T(256)(128)(2,1)S(1)} %dynamic-update-slice.1), channel_id=1, replica_groups=mesh['dp'=8,'mp'=4] {'dp'}, use_global_device_ids=true, to_apply=%add | all-reduce | flops 256 | bytes 1024
  69.1 26.4 %all-gather.10.cloned.1.call-done = bf16[2048,256]{1,0:T(8,128)(2,1)} async-done(((bf16[256,256]{1,0:T(8,128)(2,1)}), bf16[2048,256]{1,0:T(8,128)(2,1)}) %all-gather.10.cloned.1.call-update) | async-done | bytes 1048592 | tf_op jit(solution)/shard_map/all_gather | solution.py:119
  99.5 46.8 %all-gather.14.cloned.1.call-done = bf16[2048,512]{1,0:T(8,128)(2,1)} async-done(((bf16[256,512]{1,0:T(8,128)(2,1)}), bf16[2048,512]{1,0:T(8,128)(2,1)}) %all-gather.14.cloned.1.call-update) | async-done | bytes 2097168 | tf_op jit(solution)/shard_map/all_gather | solution.py:117
  164.0 34.4 %all-gather.16.cloned.1.call-done = bf16[512,2048]{1,0:T(8,128)(2,1)} async-done(((bf16[512,256]{1,0:T(8,128)(2,1)}), bf16[512,2048]{1,0:T(8,128)(2,1)}) %all-gather.16.cloned.1.call-update) | async-done | bytes 2097168 | tf_op jit(solution)/shard_map/all_gather | solution.py:120
  212.0 17.4 %all-gather.1 = bf16[8,1,256]{2,1,0:T(2,128)(2,1)S(1)} all-gather(bf16[1,1,256]{2,1,0:T(2,128)(2,1)S(1)} %reshape.306), channel_id=1, replica_groups=mesh['dp'=8,'mp'=4] {'dp'}, dimensions={0}, use_global_device_ids=true | all-gather | bytes 4608 | tf_op jit(solution)/shard_map/all_gather | solution.py:132
  230.0 126.9 %all-reduce.14.cloned.1.call-done = f32[1024,2048]{1,0:T(8,128)} async-done(((f32[1024,2048]{1,0:T(8,128)}), f32[1024,2048]{1,0:T(8,128)}) %all-reduce.14.cloned.1.call-update) | async-done | bytes 8388624 | tf_op jit(solution)/shard_map/psum | solution.py:190
  368.6 90.1 %all-gather.18.cloned.1.call-done = bf16[2048,1536]{1,0:T(8,128)(2,1)} async-done(((bf16[256,1536]{1,0:T(8,128)(2,1)}), bf16[2048,1536]{1,0:T(8,128)(2,1)}) %all-gather.18.cloned.1.call-update) | async-done | bytes 6291472 | tf_op jit(solution)/shard_map/all_gather | solution.py:133
  458.7 11.9 fusion.78
  470.6 88.1 %all-gather.20.cloned.1.call-done = bf16[2048,1536]{1,0:T(8,128)(2,1)} async-done(((bf16[256,1536]{1,0:T(8,128)(2,1)}), bf16[2048,1536]{1,0:T(8,128)(2,1)}) %all-gather.20.cloned.1.call-update) | async-done | bytes 6291472 | tf_op jit(solution)/shard_map/all_gather | solution.py:134
  558.7 11.7 fusion.79
  570.4 89.1 %all-gather.22.cloned.1.call-done = bf16[1536,2048]{1,0:T(8,128)(2,1)} async-done(((bf16[1536,256]{1,0:T(8,128)(2,1)}), bf16[1536,2048]{1,0:T(8,128)(2,1)}) %all-gather.22.cloned.1.call-update) | async-done | bytes 6291472 | tf_op jit(solution)/shard_map/all_gather | solution.py:135
  659.4 16.4 %multiply_convert_fusion.2 = (bf16[1024,1536]{1,0:T(8,128)(2,1)}, bf16[1024,1536]{1,0:T(8,128)(2,1)S(1)}, bf16[1024,1536]{1,0:T(8,128)(2,1)}) fusion(f32[1024,1536]{1,0:T(8,128)} %fusion.78, f32[1024,1536]{1,0:T(8,128)} %fusion.79, bf16[1024,2048]{1,0:T(8,128)(2,1)} %param.16, bf16[1536,2048]{1,0:T(8,128)(2,1)} %all-gather.22.cloned.1.call-done), kind=kOutput, calls=%fused_computation.43 | convolution fusion | flops 6466043904 | bytes 32505856 | tf_op jit(solution)/shard_map/dot_general | solution.py:65
  696.2 11.3 convolution_convert_fusion.3
  707.5 72.4 %all-reduce.16.cloned.1.call-done = bf16[1024,2048]{1,0:T(8,128)(2,1)} async-done(((bf16[1024,2048]{1,0:T(8,128)(2,1)}), bf16[1024,2048]{1,0:T(8,128)(2,1)}) %all-reduce.16.cloned.1.call-update) | async-done | bytes 4194320 | tf_op jit(solution)/shard_map/psum | solution.py:216
  865.8 11.5 convolution_convert_fusion.2
  906.1 146.2 %all-reduce.18.cloned.1.call-done = (bf16[1024,2048]{1,0:T(8,128)(2,1)}, bf16[1024,2048]{1,0:T(8,128)(2,1)}) async-done(((bf16[1024,2048]{1,0:T(8,128)(2,1)}, bf16[1024,2048]{1,0:T(8,128)(2,1)}), (bf16[1024,2048]{1,0:T(8,128)(2,1)}, bf16[1024,2048]{1,0:T(8,128)(2,1)})) %all-reduce.18.cloned.1.call-update) | async-done | bytes 8388624 | tf_op jit(solution)/shard_map/psum | solution.py:201
  1058.8 22.0 %all-reduce.6 = (bf16[2048]{0:T(1024)(128)(2,1)S(1)}, bf16[128]{0:T(256)(128)(2,1)S(1)}, bf16[128]{0:T(256)(128)(2,1)S(1)}, bf16[2048]{0:T(1024)(128)(2,1)S(1)}) all-reduce(bf16[2048]{0:T(1024)(128)(2,1)S(1)} %get-tuple-element.84, bf16[128]{0:T(256)(128)(2,1)S(1)} %reduce_sum.170, ...), channel_id=2, replica_groups=mesh['dp'=8,'mp'=4] {'dp'}, use_global_device_ids=true, to_apply=%region_21.22.clone | all-reduce | flops 4352 | bytes 17408
  1081.0 38.8 %reduce-scatter.10.cloned.1.call-done = bf16[256,256]{1,0:T(8,128)(2,1)} async-done(((bf16[2048,256]{1,0:T(8,128)(2,1)}), bf16[256,256]{1,0:T(8,128)(2,1)}) %reduce-scatter.10.cloned.1.call-update) | async-done | bytes 131088 | tf_op jit(solution)/shard_map/reduce_scatter | solution.py:315
  1134.7 56.6 %reduce-scatter.8.cloned.1.call-done = bf16[256,512]{1,0:T(8,128)(2,1)} async-done(((bf16[2048,512]{1,0:T(8,128)(2,1)}), bf16[256,512]{1,0:T(8,128)(2,1)}) %reduce-scatter.8.cloned.1.call-update) | async-done | bytes 262160 | tf_op jit(solution)/shard_map/reduce_scatter | solution.py:312
  1193.1 69.3 %reduce-scatter.14.cloned.1.call-done = bf16[512,256]{1,0:T(8,128)(2,1)} async-done(((bf16[512,2048]{1,0:T(8,128)(2,1)}), bf16[512,256]{1,0:T(8,128)(2,1)}) %reduce-scatter.14.cloned.1.call-update) | async-done | bytes 262160 | tf_op jit(solution)/shard_map/reduce_scatter | solution.py:321
  1273.3 110.0 %reduce-scatter.16.cloned.1.call-done = bf16[256,1536]{1,0:T(8,128)(2,1)} async-done(((bf16[2048,1536]{1,0:T(8,128)(2,1)}), bf16[256,1536]{1,0:T(8,128)(2,1)}) %reduce-scatter.16.cloned.1.call-update) | async-done | bytes 786448 | tf_op jit(solution)/shard_map/reduce_scatter | solution.py:329
  1385.7 118.5 %reduce-scatter.18.cloned.1.call-done = bf16[256,1536]{1,0:T(8,128)(2,1)} async-done(((bf16[2048,1536]{1,0:T(8,128)(2,1)}), bf16[256,1536]{1,0:T(8,128)(2,1)}) %reduce-scatter.18.cloned.1.call-update) | async-done | bytes 786448 | tf_op jit(solution)/shard_map/reduce_scatter | solution.py:332
  1506.7 119.0 %reduce-scatter.20.cloned.1.call-done = bf16[1536,256]{1,0:T(8,128)(2,1)} async-done(((bf16[1536,2048]{1,0:T(8,128)(2,1)}), bf16[1536,256]{1,0:T(8,128)(2,1)}) %reduce-scatter.20.cloned.1.call-update) | async-done | bytes 786448 | tf_op jit(solution)/shard_map/reduce_scatter | solution.py:335
  (281 shorter events, 243.5 us)
Async XLA Ops:
  7.2 56.4 %all-gather.12.cloned.1.call-start = ((), (), s32[]{:S(2)}) async-start(), calls=%async_computation.8 | async-start | bytes 1179648 | tf_op jit(solution)/shard_map/all_gather | solution.py:118
  8.9 86.6 %all-gather.10.cloned.1.call-start = ((), (), s32[]{:S(2)}) async-start(), calls=%async_computation.7 | async-start | bytes 1179648 | tf_op jit(solution)/shard_map/all_gather | solution.py:119
  10.6 52.3 %copy-start.39 = (s32[1,1024]{1,0:T(1,128)S(1)}, s32[1,1024]{1,0:T(1,128)}, u32[]{:S(2)}) copy-start(s32[1,1024]{1,0:T(1,128)} %param.15) | copy-start | bytes 12292
  10.6 135.7 %all-gather.14.cloned.1.call-start = ((), (), s32[]{:S(2)}) async-start(), calls=%async_computation.9 | async-start | bytes 2359296 | tf_op jit(solution)/shard_map/all_gather | solution.py:117
  12.5 185.9 %all-gather.16.cloned.1.call-start = ((), (), s32[]{:S(2)}) async-start(), calls=%async_computation.10 | async-start | bytes 2359296 | tf_op jit(solution)/shard_map/all_gather | solution.py:120
  14.3 342.5 %all-reduce.14.cloned.1.call-start = ((), (), s32[]{:S(2)}) async-start(), calls=%async_computation.11 | async-start | bytes 16777216 | tf_op jit(solution)/shard_map/psum | solution.py:190
  38.9 107.4 %copy-start.37 = (f32[8,1,256]{2,1,0:T(1,128)}, f32[8,1,256]{2,1,0:T(1,128)S(1)}, u32[]{:S(2)}) copy-start(f32[8,1,256]{2,1,0:T(1,128)S(1)} %convert_element_type.295) | copy-start | bytes 24580
  42.0 104.3 %copy-start.40 = (f32[1024]{0:T(1024)}, f32[1024]{0:T(1024)S(1)}, u32[]{:S(2)}) copy-start(f32[1024]{0:T(1024)S(1)} %add_rsqrt_fusion.3) | copy-start | bytes 12292
  62.9 89.5 %copy-start.7 = (f32[1024,128]{0,1:T(8,128)}, f32[1024,128]{0,1:T(8,128)S(1)}, u32[]{:S(2)}) copy-start(f32[1024,128]{0,1:T(8,128)S(1)} %pad_maximum_fusion.4) | copy-start | bytes 1572868
  62.9 89.4 %copy-start.9 = (f32[1024,128]{0,1:T(8,128)}, f32[1024,128]{0,1:T(8,128)S(1)}, u32[]{:S(2)}) copy-start(f32[1024,128]{0,1:T(8,128)S(1)} %pad_maximum_fusion.5) | copy-start | bytes 1572868
  69.1 88.1 %copy-start.16 = (bf16[1024,2,128,1]{0,2,3,1:T(8,128)(2,1)}, bf16[1024,2,128,1]{0,2,3,1:T(8,128)(2,1)S(1)}, u32[]{:S(2)}) copy-start(bf16[1024,2,128,1]{0,2,3,1:T(8,128)(2,1)S(1)} %fusion.64) | copy-start | bytes 1572868
  163.9 41.7 %copy-start.33 = (bf16[1024,2,2,128]{0,3,2,1:T(8,128)(2,1)}, bf16[1024,2,2,128]{0,3,2,1:T(8,128)(2,1)S(1)}, u32[]{:S(2)}) copy-start(bf16[1024,2,2,128]{0,3,2,1:T(8,128)(2,1)S(1)} %pad_maximum_fusion.3) | copy-start | bytes 3145732
  205.6 253.0 %all-gather.18.cloned.1.call-start = ((), (), s32[]{:S(2)}) async-start(), calls=%async_computation.12 | async-start | bytes 7077888 | tf_op jit(solution)/shard_map/all_gather | solution.py:133
  208.0 350.7 %all-gather.20.cloned.1.call-start = ((), (), s32[]{:S(2)}) async-start(), calls=%async_computation.13 | async-start | bytes 7077888 | tf_op jit(solution)/shard_map/all_gather | solution.py:134
  210.8 448.6 %all-gather.22.cloned.1.call-start = ((), (), s32[]{:S(2)}) async-start(), calls=%async_computation.14 | async-start | bytes 7077888 | tf_op jit(solution)/shard_map/all_gather | solution.py:135
  211.9 568.0 %all-reduce.16.cloned.1.call-start = ((), (), s32[]{:S(2)}) async-start(), calls=%async_computation.15 | async-start | bytes 8388608 | tf_op jit(solution)/shard_map/psum | solution.py:216
  696.1 208.3 %reduce-scatter.12.cloned.1.call-start = ((), (), s32[]{:S(2)}) async-start(), calls=%async_computation.18 | async-start | bytes 1179648 | tf_op jit(solution)/shard_map/reduce_scatter | solution.py:318
  833.7 218.6 %all-reduce.18.cloned.1.call-start = ((), (), s32[]{:S(2)}) async-start(), calls=%async_computation.23 | async-start | bytes 16777216 | tf_op jit(solution)/shard_map/psum | solution.py:201
  846.7 273.0 %reduce-scatter.10.cloned.1.call-start = ((), (), s32[]{:S(2)}) async-start(), calls=%async_computation.17 | async-start | bytes 1179648 | tf_op jit(solution)/shard_map/reduce_scatter | solution.py:315
  851.7 339.5 %reduce-scatter.8.cloned.1.call-start = ((), (), s32[]{:S(2)}) async-start(), calls=%async_computation.16 | async-start | bytes 2359296 | tf_op jit(solution)/shard_map/reduce_scatter | solution.py:312
  858.3 404.0 %reduce-scatter.14.cloned.1.call-start = ((), (), s32[]{:S(2)}) async-start(), calls=%async_computation.19 | async-start | bytes 2359296 | tf_op jit(solution)/shard_map/reduce_scatter | solution.py:321
  865.7 517.5 %reduce-scatter.16.cloned.1.call-start = ((), (), s32[]{:S(2)}) async-start(), calls=%async_computation.20 | async-start | bytes 7077888 | tf_op jit(solution)/shard_map/reduce_scatter | solution.py:329
  877.3 627.0 %reduce-scatter.18.cloned.1.call-start = ((), (), s32[]{:S(2)}) async-start(), calls=%async_computation.21 | async-start | bytes 7077888 | tf_op jit(solution)/shard_map/reduce_scatter | solution.py:332
  890.2 735.5 %reduce-scatter.20.cloned.1.call-start = ((), (), s32[]{:S(2)}) async-start(), calls=%async_computation.22 | async-start | bytes 7077888 | tf_op jit(solution)/shard_map/reduce_scatter | solution.py:335
  (52 other events, 299.5 us)
Sparse Core Ops, SparseCore 0:
  10.7 42.9 all-gather.11
  56.4 39.0 all-gather.9
  98.2 48.0 all-gather.13
  148.8 49.5 all-gather.15
  205.8 151.0 all-reduce.13
  359.5 99.1 all-gather.17
  461.4 97.1 all-gather.19
  561.3 98.1 all-gather.21
  696.2 83.6 all-reduce.15
  833.8 63.5 reduce-scatter.11
  900.0 152.2 all-reduce.17
  1056.1 63.6 reduce-scatter.9
  1124.3 66.9 reduce-scatter.7
  1195.0 67.2 reduce-scatter.13
  1266.2 117.0 reduce-scatter.15
  1387.1 117.0 reduce-scatter.17
  1508.2 117.5 reduce-scatter.19
where the time goes:
time: 1650 us; the launch traced here: 1640 us
  waiting for transfers between devices  1230 us (75%)
  matrix products  182 us (11%)
  other arithmetic  98.9 us (6%)
  blocking collectives  84.5 us (5%)
  local copies, waits for them, and re-layouts  17.7 us (1%)
  between operations  17.4 us (1%)
    psum x1, waiting for transfers between devices, on_device(): lax.psum(mlp_part.astype(jnp.bfloat16), 'mp').astype(jnp.float32)  146 us
    psum x1, waiting for transfers between devices, on_device(): hidden = inputs + lax.psum(attn_part, 'mp')  127 us
    reduce_scatter x1, waiting for transfers between devices, on_device(): lax.psum_scatter(down_grad.astype(jnp.bfloat16), 'dp', scatter_dimension=...  119 us
    reduce_scatter x1, waiting for transfers between devices, on_device(): lax.psum_scatter(up_grad.astype(jnp.bfloat16), 'dp', scatter_dimension=0,...  119 us
    reduce_scatter x1, waiting for transfers between devices, on_device(): lax.psum_scatter(gate_grad.astype(jnp.bfloat16), 'dp', scatter_dimension=...  110 us
    all_gather x1, waiting for transfers between devices, on_device(): lax.all_gather(gate_weight.astype(jnp.bfloat16), 'dp', axis=0, tiled=True)  90.1 us
    all_gather x1, waiting for transfers between devices, on_device(): lax.all_gather(down_weight.astype(jnp.bfloat16), 'dp', axis=1, tiled=True)  89.1 us
    all_gather x1, waiting for transfers between devices, on_device(): lax.all_gather(up_weight.astype(jnp.bfloat16), 'dp', axis=0, tiled=True)  88.1 us
  transfers between devices with their start and end apart: 17, of which 15 were waited for; matrix products, arithmetic and copies ran while one was open for 11% of the time, Pallas kernels for 0%

commit v1 on v0

--- a/solution.py
+++ b/solution.py
@@ -187,7 +187,7 @@
     )
     attended_flat = attention_output.reshape(rows, local_heads * head_size).astype(jnp.bfloat16)
     attn_part = jnp.dot(attended_flat, output_mat, preferred_element_type=jnp.float32)
-    hidden = inputs + lax.psum(attn_part, "mp")
+    hidden = inputs + jnp.sum(lax.all_gather(attn_part, "mp"), axis=0)
     hat_two, inv_two = norm_parts(hidden)
     normed_two = (hat_two * gain_two).astype(jnp.bfloat16)
     hidden_share = take(hidden)

time: 1650 us -> 1690 us (1.024)
  other arithmetic: 98.9 us -> 125 us
  waiting for transfers between devices: 1230 us -> 1250 us
    all_gather x0 -> x1, waiting for transfers between devices: none -> 176 us  [on_device(): hidden = inputs + jnp.sum(lax.all_gather(attn_part, 'mp'), axis=0)]
    psum x1 -> x0, waiting for transfers between devices: 127 us -> none  [on_device(): hidden = inputs + lax.psum(attn_part, 'mp')]
    all_gather x1, waiting for transfers between devices: 90.1 us -> 63 us  [on_device(): lax.all_gather(gate_weight.astype(jnp.bfloat16), 'dp', axis=0, tiled=True)]
    reduce_sum x0 -> x1, other arithmetic: none -> 26.9 us  [on_device(): hidden = inputs + jnp.sum(lax.all_gather(attn_part, 'mp'), axis=0)]
  transfers between devices with their start and end apart: 17 -> 17, of which waited for: 15 -> 15; matrix products, arithmetic and copies ran while one was open for 11% -> 13% of each run, Pallas kernels for 0% -> 0%
where the time goes in v1:
time: 1690 us; the launch traced here: 1680 us
  waiting for transfers between devices  1250 us (74%)
  matrix products  182 us (11%)
  other arithmetic  125 us (7%)
  blocking collectives  84.8 us (5%)
  local copies, waits for them, and re-layouts  17.7 us (1%)
  between operations  17.5 us (1%)
    all_gather x1, waiting for transfers between devices, on_device(): hidden = inputs + jnp.sum(lax.all_gather(attn_part, 'mp'), axis=0)  176 us
    psum x1, waiting for transfers between devices, on_device(): lax.psum(mlp_part.astype(jnp.bfloat16), 'mp').astype(jnp.float32)  146 us
    reduce_scatter x1, waiting for transfers between devices, on_device(): lax.psum_scatter(down_grad.astype(jnp.bfloat16), 'dp', scatter_dimension=...  119 us
    reduce_scatter x1, waiting for transfers between devices, on_device(): lax.psum_scatter(up_grad.astype(jnp.bfloat16), 'dp', scatter_dimension=0,...  119 us
    reduce_scatter x1, waiting for transfers between devices, on_device(): lax.psum_scatter(gate_grad.astype(jnp.bfloat16), 'dp', scatter_dimension=...  110 us
    all_gather x1, waiting for transfers between devices, on_device(): lax.all_gather(down_weight.astype(jnp.bfloat16), 'dp', axis=1, tiled=True)  89 us
    all_gather x1, waiting for transfers between devices, on_device(): lax.all_gather(up_weight.astype(jnp.bfloat16), 'dp', axis=0, tiled=True)  88.3 us
    psum x1, waiting for transfers between devices, on_device(): lax.psum(normed_two_part.astype(jnp.bfloat16), 'mp').astype(jnp.float32)  72.4 us
  transfers between devices with their start and end apart: 17, of which 15 were waited for; matrix products, arithmetic and copies ran while one was open for 13% of the time, Pallas kernels for 0%

profile of v1, /device:TPU:0, one launch (start us, length us, event | category | flops | bytes accessed | tf_op | source)
XLA Modules:
  0.0 1683.8 jit_solution(16839996541469192181)
XLA Ops:
  16.6 22.3 %all-gather.1 = bf16[8,1,256]{2,1,0:T(2,128)(2,1)S(1)} all-gather(bf16[1,1,256]{2,1,0:T(2,128)(2,1)S(1)} %reshape.305), channel_id=1, replica_groups=mesh['dp'=8,'mp'=4] {'dp'}, dimensions={0}, use_global_device_ids=true | all-gather | bytes 4608 | tf_op jit(solution)/shard_map/all_gather | solution.py:114
  43.8 17.2 %all-reduce.7 = (bf16[128]{0:T(256)(128)(2,1)S(1)}, bf16[128]{0:T(256)(128)(2,1)S(1)}) all-reduce(bf16[128]{0:T(256)(128)(2,1)S(1)} %dynamic-update-slice, bf16[128]{0:T(256)(128)(2,1)S(1)} %dynamic-update-slice.1), channel_id=1, replica_groups=mesh['dp'=8,'mp'=4] {'dp'}, use_global_device_ids=true, to_apply=%add | all-reduce | flops 256 | bytes 1024
  69.1 26.4 %all-gather.12.cloned.1.call-done = bf16[2048,256]{1,0:T(8,128)(2,1)} async-done(((bf16[256,256]{1,0:T(8,128)(2,1)}), bf16[2048,256]{1,0:T(8,128)(2,1)}) %all-gather.12.cloned.1.call-update) | async-done | bytes 1048592 | tf_op jit(solution)/shard_map/all_gather | solution.py:119
  99.5 46.8 %all-gather.16.cloned.1.call-done = bf16[2048,512]{1,0:T(8,128)(2,1)} async-done(((bf16[256,512]{1,0:T(8,128)(2,1)}), bf16[2048,512]{1,0:T(8,128)(2,1)}) %all-gather.16.cloned.1.call-update) | async-done | bytes 2097168 | tf_op jit(solution)/shard_map/all_gather | solution.py:117
  163.9 34.5 %all-gather.18.cloned.1.call-done = bf16[512,2048]{1,0:T(8,128)(2,1)} async-done(((bf16[512,256]{1,0:T(8,128)(2,1)}), bf16[512,2048]{1,0:T(8,128)(2,1)}) %all-gather.18.cloned.1.call-update) | async-done | bytes 2097168 | tf_op jit(solution)/shard_map/all_gather | solution.py:120
  211.7 17.7 %all-gather.2 = bf16[8,1,256]{2,1,0:T(2,128)(2,1)S(1)} all-gather(bf16[1,1,256]{2,1,0:T(2,128)(2,1)S(1)} %reshape.307), channel_id=1, replica_groups=mesh['dp'=8,'mp'=4] {'dp'}, dimensions={0}, use_global_device_ids=true | all-gather | bytes 4608 | tf_op jit(solution)/shard_map/all_gather | solution.py:132
  230.0 175.5 %all-gather.26.cloned.1.call-done = f32[4096,2048]{1,0:T(8,128)} async-done(((f32[1024,2048]{1,0:T(8,128)}), f32[4096,2048]{1,0:T(8,128)}) %all-gather.26.cloned.1.call-update) | async-done | bytes 33554448 | tf_op jit(solution)/shard_map/all_gather | solution.py:190
  405.5 26.9 %reduce_sum.169 = f32[1024,2048]{1,0:T(8,128)} reduce(f32[4,1024,2048]{2,1,0:T(8,128)} %bitcast.223, f32[]{:T(128)} %constant.54.clone.1), dimensions={0}, to_apply=%region_9.10 | reduce | flops 6291456 | bytes 41943044 | tf_op jit(solution)/shard_map/reduce_sum | solution.py:190
  444.2 63.0 %all-gather.20.cloned.1.call-done = bf16[2048,1536]{1,0:T(8,128)(2,1)} async-done(((bf16[256,1536]{1,0:T(8,128)(2,1)}), bf16[2048,1536]{1,0:T(8,128)(2,1)}) %all-gather.20.cloned.1.call-update) | async-done | bytes 6291472 | tf_op jit(solution)/shard_map/all_gather | solution.py:133
  507.2 11.7 fusion.78
  518.8 88.3 %all-gather.22.cloned.1.call-done = bf16[2048,1536]{1,0:T(8,128)(2,1)} async-done(((bf16[256,1536]{1,0:T(8,128)(2,1)}), bf16[2048,1536]{1,0:T(8,128)(2,1)}) %all-gather.22.cloned.1.call-update) | async-done | bytes 6291472 | tf_op jit(solution)/shard_map/all_gather | solution.py:134
  607.2 11.8 fusion.79
  619.0 89.0 %all-gather.24.cloned.1.call-done = bf16[1536,2048]{1,0:T(8,128)(2,1)} async-done(((bf16[1536,256]{1,0:T(8,128)(2,1)}), bf16[1536,2048]{1,0:T(8,128)(2,1)}) %all-gather.24.cloned.1.call-update) | async-done | bytes 6291472 | tf_op jit(solution)/shard_map/all_gather | solution.py:135
  708.0 16.4 multiply_convert_fusion.2
  756.1 72.4 %all-reduce.13.cloned.1.call-done = bf16[1024,2048]{1,0:T(8,128)(2,1)} async-done(((bf16[1024,2048]{1,0:T(8,128)(2,1)}), bf16[1024,2048]{1,0:T(8,128)(2,1)}) %all-reduce.13.cloned.1.call-update) | async-done | bytes 4194320 | tf_op jit(solution)/shard_map/psum | solution.py:216
  914.4 11.5 convolution_convert_fusion.2
  954.7 146.2 %all-reduce.15.cloned.1.call-done = (bf16[1024,2048]{1,0:T(8,128)(2,1)}, bf16[1024,2048]{1,0:T(8,128)(2,1)}) async-done(((bf16[1024,2048]{1,0:T(8,128)(2,1)}, bf16[1024,2048]{1,0:T(8,128)(2,1)}), (bf16[1024,2048]{1,0:T(8,128)(2,1)}, bf16[1024,2048]{1,0:T(8,128)(2,1)})) %all-reduce.15.cloned.1.call-update) | async-done | bytes 8388624 | tf_op jit(solution)/shard_map/psum | solution.py:201
  1107.5 22.0 %all-reduce.6 = (bf16[2048]{0:T(1024)(128)(2,1)S(1)}, bf16[128]{0:T(256)(128)(2,1)S(1)}, bf16[128]{0:T(256)(128)(2,1)S(1)}, bf16[2048]{0:T(1024)(128)(2,1)S(1)}) all-reduce(bf16[2048]{0:T(1024)(128)(2,1)S(1)} %get-tuple-element.84, bf16[128]{0:T(256)(128)(2,1)S(1)} %reduce_sum.180, ...), channel_id=3, replica_groups=mesh['dp'=8,'mp'=4] {'dp'}, use_global_device_ids=true, to_apply=%region_21.22.clone | all-reduce | flops 4352 | bytes 17408
  1129.7 38.8 %reduce-scatter.10.cloned.1.call-done = bf16[256,256]{1,0:T(8,128)(2,1)} async-done(((bf16[2048,256]{1,0:T(8,128)(2,1)}), bf16[256,256]{1,0:T(8,128)(2,1)}) %reduce-scatter.10.cloned.1.call-update) | async-done | bytes 131088 | tf_op jit(solution)/shard_map/reduce_scatter | solution.py:315
  1183.3 56.7 %reduce-scatter.8.cloned.1.call-done = bf16[256,512]{1,0:T(8,128)(2,1)} async-done(((bf16[2048,512]{1,0:T(8,128)(2,1)}), bf16[256,512]{1,0:T(8,128)(2,1)}) %reduce-scatter.8.cloned.1.call-update) | async-done | bytes 262160 | tf_op jit(solution)/shard_map/reduce_scatter | solution.py:312
  1241.8 69.3 %reduce-scatter.14.cloned.1.call-done = bf16[512,256]{1,0:T(8,128)(2,1)} async-done(((bf16[512,2048]{1,0:T(8,128)(2,1)}), bf16[512,256]{1,0:T(8,128)(2,1)}) %reduce-scatter.14.cloned.1.call-update) | async-done | bytes 262160 | tf_op jit(solution)/shard_map/reduce_scatter | solution.py:321
  1322.1 109.9 %reduce-scatter.16.cloned.1.call-done = bf16[256,1536]{1,0:T(8,128)(2,1)} async-done(((bf16[2048,1536]{1,0:T(8,128)(2,1)}), bf16[256,1536]{1,0:T(8,128)(2,1)}) %reduce-scatter.16.cloned.1.call-update) | async-done | bytes 786448 | tf_op jit(solution)/shard_map/reduce_scatter | solution.py:329
  1434.4 118.5 %reduce-scatter.18.cloned.1.call-done = bf16[256,1536]{1,0:T(8,128)(2,1)} async-done(((bf16[2048,1536]{1,0:T(8,128)(2,1)}), bf16[256,1536]{1,0:T(8,128)(2,1)}) %reduce-scatter.18.cloned.1.call-update) | async-done | bytes 786448 | tf_op jit(solution)/shard_map/reduce_scatter | solution.py:332
  1555.4 119.0 %reduce-scatter.20.cloned.1.call-done = bf16[1536,256]{1,0:T(8,128)(2,1)} async-done(((bf16[1536,2048]{1,0:T(8,128)(2,1)}), bf16[1536,256]{1,0:T(8,128)(2,1)}) %reduce-scatter.20.cloned.1.call-update) | async-done | bytes 786448 | tf_op jit(solution)/shard_map/reduce_scatter | solution.py:335
  (286 shorter events, 254.5 us)
Async XLA Ops:
  7.2 56.5 %all-gather.14.cloned.1.call-start = ((), (), s32[]{:S(2)}) async-start(), calls=%async_computation.8 | async-start | bytes 1179648 | tf_op jit(solution)/shard_map/all_gather | solution.py:118
  8.9 86.6 %all-gather.12.cloned.1.call-start = ((), (), s32[]{:S(2)}) async-start(), calls=%async_computation.7 | async-start | bytes 1179648 | tf_op jit(solution)/shard_map/all_gather | solution.py:119
  10.6 52.4 %copy-start.39 = (s32[1,1024]{1,0:T(1,128)S(1)}, s32[1,1024]{1,0:T(1,128)}, u32[]{:S(2)}) copy-start(s32[1,1024]{1,0:T(1,128)} %param.15) | copy-start | bytes 12292
  10.6 135.7 %all-gather.16.cloned.1.call-start = ((), (), s32[]{:S(2)}) async-start(), calls=%async_computation.9 | async-start | bytes 2359296 | tf_op jit(solution)/shard_map/all_gather | solution.py:117
  12.5 185.9 %all-gather.18.cloned.1.call-start = ((), (), s32[]{:S(2)}) async-start(), calls=%async_computation.10 | async-start | bytes 2359296 | tf_op jit(solution)/shard_map/all_gather | solution.py:120
  14.3 391.2 %all-gather.26.cloned.1.call-start = ((), (), s32[]{:S(2)}) async-start(), calls=%async_computation.22 | async-start | bytes 41943040 | tf_op jit(solution)/shard_map/all_gather | solution.py:190
  38.9 107.4 %copy-start.37 = (f32[8,1,256]{2,1,0:T(1,128)}, f32[8,1,256]{2,1,0:T(1,128)S(1)}, u32[]{:S(2)}) copy-start(f32[8,1,256]{2,1,0:T(1,128)S(1)} %convert_element_type.295) | copy-start | bytes 24580
  42.0 104.3 %copy-start.40 = (f32[1024]{0:T(1024)}, f32[1024]{0:T(1024)S(1)}, u32[]{:S(2)}) copy-start(f32[1024]{0:T(1024)S(1)} %add_rsqrt_fusion.3) | copy-start | bytes 12292
  62.9 89.5 %copy-start.7 = (f32[1024,128]{0,1:T(8,128)}, f32[1024,128]{0,1:T(8,128)S(1)}, u32[]{:S(2)}) copy-start(f32[1024,128]{0,1:T(8,128)S(1)} %pad_maximum_fusion.4) | copy-start | bytes 1572868
  62.9 89.4 %copy-start.9 = (f32[1024,128]{0,1:T(8,128)}, f32[1024,128]{0,1:T(8,128)S(1)}, u32[]{:S(2)}) copy-start(f32[1024,128]{0,1:T(8,128)S(1)} %pad_maximum_fusion.5) | copy-start | bytes 1572868
  62.9 166.5 %copy-start.42 = (f32[128]{0:T(128)}, f32[128]{0:T(128)S(1)}, u32[]{:S(2)}) copy-start(f32[128]{0:T(128)S(1)} %convert_element_type.238) | copy-start | bytes 1540
  69.1 88.0 %copy-start.16 = (bf16[1024,2,128,1]{0,2,3,1:T(8,128)(2,1)}, bf16[1024,2,128,1]{0,2,3,1:T(8,128)(2,1)S(1)}, u32[]{:S(2)}) copy-start(bf16[1024,2,128,1]{0,2,3,1:T(8,128)(2,1)S(1)} %fusion.64) | copy-start | bytes 1572868
  205.7 301.5 %all-gather.20.cloned.1.call-start = ((), (), s32[]{:S(2)}) async-start(), calls=%async_computation.11 | async-start | bytes 7077888 | tf_op jit(solution)/shard_map/all_gather | solution.py:133
  208.0 399.2 %all-gather.22.cloned.1.call-start = ((), (), s32[]{:S(2)}) async-start(), calls=%async_computation.12 | async-start | bytes 7077888 | tf_op jit(solution)/shard_map/all_gather | solution.py:134
  210.6 497.4 %all-gather.24.cloned.1.call-start = ((), (), s32[]{:S(2)}) async-start(), calls=%async_computation.13 | async-start | bytes 7077888 | tf_op jit(solution)/shard_map/all_gather | solution.py:135
  211.6 616.9 %all-reduce.13.cloned.1.call-start = ((), (), s32[]{:S(2)}) async-start(), calls=%async_computation.14 | async-start | bytes 8388608 | tf_op jit(solution)/shard_map/psum | solution.py:216
  744.7 208.4 %reduce-scatter.12.cloned.1.call-start = ((), (), s32[]{:S(2)}) async-start(), calls=%async_computation.17 | async-start | bytes 1179648 | tf_op jit(solution)/shard_map/reduce_scatter | solution.py:318
  882.3 218.7 %all-reduce.15.cloned.1.call-start = ((), (), s32[]{:S(2)}) async-start(), calls=%async_computation.23 | async-start | bytes 16777216 | tf_op jit(solution)/shard_map/psum | solution.py:201
  895.4 273.1 %reduce-scatter.10.cloned.1.call-start = ((), (), s32[]{:S(2)}) async-start(), calls=%async_computation.16 | async-start | bytes 1179648 | tf_op jit(solution)/shard_map/reduce_scatter | solution.py:315
  900.4 339.6 %reduce-scatter.8.cloned.1.call-start = ((), (), s32[]{:S(2)}) async-start(), calls=%async_computation.15 | async-start | bytes 2359296 | tf_op jit(solution)/shard_map/reduce_scatter | solution.py:312
  907.0 404.2 %reduce-scatter.14.cloned.1.call-start = ((), (), s32[]{:S(2)}) async-start(), calls=%async_computation.18 | async-start | bytes 2359296 | tf_op jit(solution)/shard_map/reduce_scatter | solution.py:321
  914.4 517.6 %reduce-scatter.16.cloned.1.call-start = ((), (), s32[]{:S(2)}) async-start(), calls=%async_computation.19 | async-start | bytes 7077888 | tf_op jit(solution)/shard_map/reduce_scatter | solution.py:329
  925.9 627.0 %reduce-scatter.18.cloned.1.call-start = ((), (), s32[]{:S(2)}) async-start(), calls=%async_computation.20 | async-start | bytes 7077888 | tf_op jit(solution)/shard_map/reduce_scatter | solution.py:332
  938.9 735.5 %reduce-scatter.20.cloned.1.call-start = ((), (), s32[]{:S(2)}) async-start(), calls=%async_computation.21 | async-start | bytes 7077888 | tf_op jit(solution)/shard_map/reduce_scatter | solution.py:335
  (54 other events, 342.9 us)
Sparse Core Ops, SparseCore 0:
  10.7 42.9 all-gather.13
  56.4 39.0 all-gather.11
  98.2 48.0 all-gather.15
  148.8 49.5 all-gather.17
  205.8 199.6 all-gather.25
  408.1 99.0 all-gather.19
  509.9 97.1 all-gather.21
  609.8 98.1 all-gather.23
  744.8 83.6 all-reduce.12
  882.4 63.6 reduce-scatter.11
  948.7 152.2 all-reduce.14
  1104.8 63.6 reduce-scatter.9
  1173.0 66.9 reduce-scatter.7
  1243.8 67.2 reduce-scatter.13
  1315.0 116.9 reduce-scatter.15
  1435.8 117.0 reduce-scatter.17
  1556.8 117.5 reduce-scatter.19
